TPU v7x, 32 devices: a whole 2x2x4 slice. The times are simulated.
32 devices in a mesh: groups: 2 (over y), seq: 4 (over z), blk: 2 (over x), chan: 2 (over core).
Axes of the slice: x: 2, y: 2, z: 4, core: 2. Of those that a mesh axis runs over, the one named last changes fastest.
Arguments:
- queries: bfloat16 [4, 8, 32, 4096], P(('groups', 'blk'), 'seq', 'chan'), parts along dimension 0, may hold values from -8 to 8
- keys: bfloat16 [4, 8, 32, 4096], P(('groups', 'blk'), 'seq', 'chan'), parts along dimension 0, may hold values from -8 to 8
- values: bfloat16 [4, 8, 32, 4096], P(('groups', 'blk'), 'seq', 'chan'), parts along dimension 0, may hold values from -16 to 16
- norm_gain: float32 [4096], replicated, may hold values from 0.1 to 1.9
- head_weight: bfloat16 [4096, 64], replicated, may hold values from -0.09375 to 0.09375
- head_bias: float32 [64], replicated, may hold values from -3 to 3
- in_weight: bfloat16 [3, 3, 64, 512], replicated, may hold values from -0.25 to 0.25
- in_bias: float32 [512], replicated, may hold values from -3 to 3
- conv_weight: bfloat16 [3, 3, 512, 512], P(None, None, None, 'chan'), may hold values from -0.15625 to 0.15625
- conv_bias: float32 [512], P('chan'), may hold values from -3 to 3
Outputs:
- decoded: bfloat16 [4, 8, 32, 512], P(('groups', 'blk'), 'seq', None, 'chan'), parts along dimension 0
There are 2 independent parts, one for each index of `groups`. A program takes and returns all parts, laid end to end along the dimension named above; an argument that names none is the same for every part. Nothing has to cross between parts.
All inputs are finite; a program needn't handle non-finite values.
Results may differ from a plain program's by a relative error of at most 0.025.
Values may be sent and summed in bfloat16 or wider, within the bound.
No kernel may reach another device: no remote copies, remote signals or barrier semaphores. Data moves between devices by JAX's collectives and lax.ppermute only.
A program may use at most 64 MiB of HBM per device.

v0:
```python
import jax
import jax.numpy as jnp
from jax import lax
from jax.sharding import PartitionSpec as P

HD = 128
epsilon = 1e-06


def with_halo(cells, sides, width):
    for axis, dim in sides:
        count = lax.axis_size(axis)
        ends = count - 1
        head = lax.slice_in_dim(cells, 0, width, axis=dim)
        tail = lax.slice_in_dim(cells, cells.shape[dim] - width, cells.shape[dim], axis=dim)
        cells = jnp.concatenate(
            [
                lax.ppermute(tail, axis, [(i, (i + 1) % count) for i in range(ends)]),
                cells,
                lax.ppermute(head, axis, [((i + 1) % count, i) for i in range(ends)]),
            ],
            axis=dim,
        )
    return cells


def conv_valid(inputs, kernel):
    col_count = inputs.shape[2]
    padded = jnp.pad(inputs, ((0, 0), (0, 0), (1, 1), (0, 0)))
    stacked = jnp.concatenate(
        [padded[:, :, col_tap : col_tap + col_count, :] for col_tap in range(3)], axis=-1
    )
    rows_out = inputs.shape[1] - 2
    result = None
    for row_tap in range(3):
        flat_kernel = kernel[row_tap].reshape(3 * kernel.shape[2], kernel.shape[3])
        term = jnp.einsum(
            "frci,io->frco",
            stacked[:, row_tap : row_tap + rows_out],
            flat_kernel,
            preferred_element_type=jnp.float32,
        )
        result = term if result is None else result + term
    return result


def absorb(running, key_block, value_block, query_heads, score_scale):
    run_max, denoms, numers = running
    scores = (
        jnp.einsum("hqd,hkd->hqk", query_heads, key_block, preferred_element_type=jnp.float32)
        * score_scale
    )
    fresh_max = jnp.maximum(run_max, jnp.max(scores, axis=-1))
    rescale = jnp.exp(run_max - fresh_max)
    expo = jnp.exp(scores - fresh_max[..., None])
    denoms = denoms * rescale + jnp.sum(expo, axis=-1)
    numers = numers * rescale[..., None] + jnp.einsum(
        "hqk,hkd->hqd", expo.astype(jnp.bfloat16), value_block, preferred_element_type=jnp.float32
    )
    return (fresh_max, denoms, numers)


def per_device(
    queries,
    keys,
    values,
    norm_gain,
    head_weight,
    head_bias,
    in_weight,
    in_bias,
    conv_weight,
    conv_bias,
):
    frame_dev, rows_dev, cols_dev, feat = queries.shape
    seq_count = lax.axis_size("seq")
    feat_dev = feat // seq_count
    heads_dev = feat_dev // HD
    score_scale = HD ** (-0.5)
    query_all, key_all, value_all = (
        lax.all_to_all(queries, "seq", split_axis=3, concat_axis=1, tiled=True),
        lax.all_to_all(keys, "seq", split_axis=3, concat_axis=1, tiled=True),
        lax.all_to_all(values, "seq", split_axis=3, concat_axis=1, tiled=True),
    )
    all_rows = query_all.shape[1]

    def to_heads(block):
        return block.reshape(-1, heads_dev, HD).transpose(1, 0, 2)

    query_heads = to_heads(query_all)
    key_heads = to_heads(key_all)
    value_heads = to_heads(value_all)
    token_local = query_heads.shape[1]

    def attend_piece(running, block_pair):
        key_piece, value_piece = block_pair
        key_rows = key_piece.shape[1]
        if key_rows > 1024 and key_rows % 1024 == 0:
            count = key_rows // 1024
            key_split = key_piece.reshape(heads_dev, count, 1024, HD).transpose(1, 0, 2, 3)
            value_split = value_piece.reshape(heads_dev, count, 1024, HD).transpose(1, 0, 2, 3)

            def step_block(state, pair_block):
                return (absorb(state, pair_block[0], pair_block[1], query_heads, score_scale), None)

            running, _ = lax.scan(step_block, running, (key_split, value_split))
            return running
        return absorb(running, key_piece, value_piece, query_heads, score_scale)

    start_state = (
        jnp.full((heads_dev, token_local), -1e30, jnp.float32),
        jnp.zeros((heads_dev, token_local), jnp.float32),
        jnp.zeros((heads_dev, token_local, HD), jnp.float32),
    )
    run_max, denoms, numers = attend_piece(
        start_state,
        (
            lax.all_gather(key_heads, ("blk", "chan"), axis=1, tiled=True),
            lax.all_gather(value_heads, ("blk", "chan"), axis=1, tiled=True),
        ),
    )
    attended = (numers / denoms[..., None]).astype(jnp.bfloat16)
    attended = attended.transpose(1, 0, 2).reshape(frame_dev, all_rows, cols_dev, feat_dev)
    back = lax.all_to_all(attended, "seq", split_axis=1, concat_axis=3, tiled=True)
    wide_att = back.astype(jnp.float32)
    squares = jnp.sum(wide_att * wide_att, axis=-1)
    normed = (wide_att * norm_gain).astype(jnp.bfloat16)
    projected = jnp.einsum("frcd,dl->frcl", normed, head_weight, preferred_element_type=jnp.float32)
    rms = jnp.sqrt(squares / feat + epsilon)
    latent_cols = (projected / rms[..., None] + head_bias).astype(jnp.bfloat16)
    latent = lax.all_gather(latent_cols, "chan", axis=2, tiled=True)
    wide_rows = with_halo(latent, (("seq", 1),), 2)
    pre_act = conv_valid(wide_rows, in_weight) + in_bias
    row_ids = lax.axis_index("seq") * rows_dev - 1 + jnp.arange(rows_dev + 2, dtype=jnp.int32)
    inside = (row_ids >= 0) & (row_ids < rows_dev * seq_count)
    activation = jnp.where(inside[None, :, None, None], jax.nn.silu(pre_act), 0.0).astype(
        jnp.bfloat16
    )
    decoded = (conv_valid(activation, conv_weight) + conv_bias).astype(jnp.bfloat16)
    return decoded


def solution(mesh):
    return jax.shard_map(
        per_device,
        mesh=mesh,
        in_specs=(
            P(("groups", "blk"), "seq", "chan", None),
            P(("groups", "blk"), "seq", "chan", None),
            P(("groups", "blk"), "seq", "chan", None),
            P(),
            P(),
            P(),
            P(),
            P(),
            P(None, None, None, "chan"),
            P("chan"),
        ),
        out_specs=P(("groups", "blk"), "seq", None, "chan"),
        check_vma=False,
    )
```

profile of v0, /device:TPU:0, one launch (start us, length us, event | category | flops | bytes accessed | tf_op | source)
XLA Modules:
  0.0 111.8 jit_solution(7479379873750700301)
XLA Ops:
  6.5 0.0 copy-start
  6.5 0.0 all-gather.4.cloned.1.call-start
  6.5 4.5 %copy.29 = bf16[1,2,16,4096]{2,1,0,3:T(2,128)(2,1)S(1)} copy(bf16[1,2,16,4096]{3,2,1,0:T(8,128)(2,1)} %param.11) | data formatting | bytes 524288 | tf_op args[1]
  11.1 2.2 %reshape.143 = bf16[4,2,16384]{2,1,0:T(2,128)(2,1)S(1)} reshape(bf16[4096,1,2,16]{3,2,1,0:T(2,128)(2,1)S(1)} %bitcast.113) | data formatting | bytes 524288
  13.3 15.0 %all_to_all.54 = bf16[4,2,16384]{2,1,0:T(2,128)(2,1)S(1)} all-to-all(bf16[4,2,16384]{2,1,0:T(2,128)(2,1)S(1)} %reshape.143), channel_id=1, replica_groups=mesh['groups'=2,'seq'=4,'blk'=2,'chan'=2] {'seq'}, dimensions={0} | all-to-all | bytes 524288 | tf_op jit(solution)/shard_map/all_to_all | solution.py:82
  28.3 1.4 %reshape.144 = bf16[4096,1,2,16]{3,2,1,0:T(2,128)(2,1)S(1)} reshape(bf16[4,2,16384]{2,1,0:T(2,128)(2,1)S(1)} %all_to_all.54) | data formatting | bytes 524288
  29.8 0.0 copy-start.1
  29.8 1.3 %copy.30 = bf16[1,2,16,4,1024]{4,2,1,3,0:T(8,128)(2,1)S(1)} copy(bf16[1,2,16,4,1024]{2,1,4,3,0:T(2,128)(2,1)S(1)} %bitcast.110) | data formatting | bytes 524288 | tf_op jit(solution)/shard_map/all_to_all | solution.py:82
  31.1 0.7 copy.51
  31.8 0.0 all-gather.4.cloned.1.call-update
  31.8 0.0 all-gather.6.cloned.1.call-start
  31.9 0.0 copy-done.1
  31.9 2.7 %copy.32 = bf16[1,2,16,4096]{2,1,0,3:T(2,128)(2,1)S(1)} copy(bf16[1,2,16,4096]{3,2,1,0:T(8,128)(2,1)S(1)} %copy-done.1) | data formatting | bytes 524288 | tf_op args[2]
  34.7 2.2 %reshape.141 = bf16[4,2,16384]{2,1,0:T(2,128)(2,1)S(1)} reshape(bf16[4096,1,2,16]{3,2,1,0:T(2,128)(2,1)S(1)} %bitcast.114) | data formatting | bytes 524288
  36.9 11.0 %all_to_all.55 = bf16[4,2,16384]{2,1,0:T(2,128)(2,1)S(1)} all-to-all(bf16[4,2,16384]{2,1,0:T(2,128)(2,1)S(1)} %reshape.141), channel_id=1, replica_groups=mesh['groups'=2,'seq'=4,'blk'=2,'chan'=2] {'seq'}, dimensions={0} | all-to-all | bytes 524288 | tf_op jit(solution)/shard_map/all_to_all | solution.py:83
  47.8 1.4 %reshape.142 = bf16[4096,1,2,16]{3,2,1,0:T(2,128)(2,1)S(1)} reshape(bf16[4,2,16384]{2,1,0:T(2,128)(2,1)S(1)} %all_to_all.55) | data formatting | bytes 524288
  49.3 0.0 copy-start.2
  49.3 1.3 %copy.33 = bf16[1,2,16,4,1024]{4,2,1,3,0:T(8,128)(2,1)S(1)} copy(bf16[1,2,16,4,1024]{2,1,4,3,0:T(2,128)(2,1)S(1)} %bitcast.111) | data formatting | bytes 524288 | tf_op jit(solution)/shard_map/all_to_all | solution.py:83
  50.6 0.7 copy.50
  51.3 0.0 all-gather.6.cloned.1.call-update
  51.4 0.0 copy-done.2
  51.4 2.7 %copy.26 = bf16[1,2,16,4096]{2,1,0,3:T(2,128)(2,1)S(1)} copy(bf16[1,2,16,4096]{3,2,1,0:T(8,128)(2,1)S(1)} %copy-done.2) | data formatting | bytes 524288 | tf_op args[0]
  54.1 2.2 %reshape.145 = bf16[4,2,16384]{2,1,0:T(2,128)(2,1)S(1)} reshape(bf16[4096,1,2,16]{3,2,1,0:T(2,128)(2,1)S(1)} %bitcast.115) | data formatting | bytes 524288
  56.3 11.0 %all_to_all.56 = bf16[4,2,16384]{2,1,0:T(2,128)(2,1)S(1)} all-to-all(bf16[4,2,16384]{2,1,0:T(2,128)(2,1)S(1)} %reshape.145), channel_id=1, replica_groups=mesh['groups'=2,'seq'=4,'blk'=2,'chan'=2] {'seq'}, dimensions={0} | all-to-all | bytes 524288 | tf_op jit(solution)/shard_map/all_to_all | solution.py:81
  67.3 1.4 %reshape.146 = bf16[4096,1,2,16]{3,2,1,0:T(2,128)(2,1)S(1)} reshape(bf16[4,2,16384]{2,1,0:T(2,128)(2,1)S(1)} %all_to_all.56) | data formatting | bytes 524288
  68.7 1.3 %copy.27 = bf16[1,2,16,4,1024]{4,2,1,3,0:T(8,128)(2,1)S(1)} copy(bf16[1,2,16,4,1024]{2,1,4,3,0:T(2,128)(2,1)S(1)} %bitcast.112) | data formatting | bytes 524288 | tf_op jit(solution)/shard_map/all_to_all | solution.py:81
  70.1 0.0 all-gather.4.cloned.1.call-done
  70.1 1.7 %multiply_reduce_fusion = (f32[8,128]{1,0:T(8,128)S(1)}, f32[8,128,512]{2,1,0:T(8,128)S(1)}) fusion(bf16[8,512,128]{2,1,0:T(8,128)(2,1)} %all-gather.4.cloned.1.call-done, bf16[128,8,128]{2,1,0:T(8,128)(2,1)S(1)} %bitcast.127), kind=kOutput, calls=%fused_computation.1 | convolution fusion | flops 135265280 | bytes 3411968 | tf_op jit(solution)/shard_map/hqd,hkd->hqk/dot_general | solution.py:50
  71.8 0.6 fusion
  72.4 0.0 all-gather.6.cloned.1.call-done
  72.5 1.9 %fusion.4 = bf16[128,8,128]{2,0,1:T(8,128)(2,1)S(1)} fusion(bf16[8,512,128]{2,1,0:T(8,128)(2,1)} %all-gather.6.cloned.1.call-done, f32[8,128,512]{2,1,0:T(8,128)S(1)} %get-tuple-element.18, f32[8,128]{1,0:T(8,128)S(1)} %get-tuple-element.16, f32[128,8]{0,1:T(8,128)S(1)} %bitcast_add_fusion, f32[128,8]{0,1:T(8,128)S(1)} %get-tuple-element.15), kind=kOutput, calls=%fused_computation.7 | convolution fusion | flops 136183808 | bytes 3420160 | tf_op jit(solution)/shard_map/hqk,hkd->hqd/dot_general | solution.py:57
  74.4 0.2 copy.35
  74.6 0.8 reshape.124
  75.4 3.4 %all-to-all-start.3 = ((bf16[1,8,16,1024]{3,2,0,1:T(8,128)(2,1)}), bf16[1,8,16,1024]{3,2,0,1:T(8,128)(2,1)S(1)}, u32[]{:S(2)}, u32[]{:S(2)}) async-start(bf16[1,8,16,1024]{3,2,0,1:T(8,128)(2,1)} %bitcast.12), calls=%async_computation.3 | async-start | bytes 524288 | tf_op jit(solution)/shard_map/all_to_all | solution.py:124
  78.8 1.8 %fusion.30 = (bf16[1,3,64,512]{3,2,1,0:T(8,128)(2,1)}, bf16[1,3,64,512]{3,2,1,0:T(8,128)(2,1)S(1)}, bf16[1,3,64,512]{3,2,1,0:T(8,128)(2,1)S(1)}) fusion(bf16[3,3,64,512]{3,2,1,0:T(8,128)(2,1)} %param.16), kind=kLoop, calls=%fused_computation.60 | loop fusion | bytes 1179648 | tf_op jit(solution)/shard_map/slice | solution.py:36
  80.6 1.8 %fusion.29 = (bf16[1,3,512,256]{3,2,1,0:T(8,128)(2,1)S(1)}, bf16[1,3,512,256]{3,2,1,0:T(8,128)(2,1)S(1)}, bf16[1,3,512,256]{3,2,1,0:T(8,128)(2,1)S(1)}) fusion(bf16[3,3,512,256]{3,2,1,0:T(8,128)(2,1)} %param.18), kind=kLoop, calls=%fused_computation.59 | loop fusion | bytes 4718592 | tf_op jit(solution)/shard_map/slice | solution.py:36
  82.4 0.0 copy-start.4
  82.4 4.3 %all-to-all-done.3 = bf16[1,8,16,1024]{3,2,0,1:T(8,128)(2,1)S(1)} async-done(((bf16[1,8,16,1024]{3,2,0,1:T(8,128)(2,1)}), bf16[1,8,16,1024]{3,2,0,1:T(8,128)(2,1)S(1)}, u32[]{:S(2)}, u32[]{:S(2)}) %all-to-all-start.3) | async-done | bytes 262176 | tf_op jit(solution)/shard_map/all_to_all | solution.py:124
  86.8 1.1 %copy.38 = f32[1,2,16,4,1024]{4,3,2,1,0:T(4,128)} copy(f32[1,2,16,4,1024]{4,2,1,3,0:T(8,128)S(1)} %bitcast.119) | data formatting | bytes 1048576 | tf_op jit(solution)/shard_map/convert_element_type | solution.py:125
  87.9 2.2 %reshape.131 = f32[2,16,4096]{2,1,0:T(8,128)} reshape(f32[1,2,16,4,1024]{4,3,2,1,0:T(4,128)} %copy.38) | data formatting | bytes 1048576 | tf_op jit(solution)/shard_map/convert_element_type | solution.py:125
  90.1 0.7 multiply_reduce_fusion.1
  90.8 0.0 copy-start.6
  90.8 0.7 reduce_sum.31
  91.6 0.0 copy-start.3
  91.6 0.0 copy-done
  91.6 0.0 copy-done.4
  91.6 1.4 %fusion.10 = bf16[2,16,64]{2,1,0:T(8,128)(2,1)S(1)} fusion(bf16[4096,64]{0,1:T(8,128)(2,1)S(1)} %copy-done, f32[2,16,4096]{2,1,0:T(8,128)} %reshape.131, f32[4096]{0:T(1024)S(1)} %copy-done.4, f32[64]{0:T(128)} %param.15, f32[2,16]{1,0:T(2,128)S(1)} %add_sqrt_fusion), kind=kOutput, calls=%fused_computation.18 | convolution fusion | flops 17045504 | bytes 1069440 | tf_op jit(solution)/shard_map/frcd,dl->frcl/dot_general | solution.py:128
  93.0 1.8 %all-gather = bf16[2,32,64]{2,1,0:T(8,128)(2,1)S(1)} all-gather(bf16[2,16,64]{2,1,0:T(8,128)(2,1)S(1)} %fusion.10), channel_id=2, replica_groups=mesh['groups'=2,'seq'=4,'blk'=2,'chan'=2] {'chan'}, dimensions={1}, use_global_device_ids=true | all-gather | bytes 12288 | tf_op jit(solution)/shard_map/all_gather | solution.py:131
  94.8 2.2 %collective-permute-start = (bf16[1,2,32,64]{3,2,1,0:T(8,128)(2,1)S(1)}, bf16[1,2,32,64]{3,2,1,0:T(8,128)(2,1)S(1)}, u32[]{:S(2)}, u32[]{:S(2)}) collective-permute-start(bf16[1,2,32,64]{3,2,1,0:T(8,128)(2,1)S(1)} %bitcast.131), channel_id=1, source_target_pairs={{0,4},{4,8},{8,12},{1,5},{5,9},{9,13},{2,6},{6,10},{10,14},{3,7},{... | collective-permute-start | bytes 24584 | tf_op jit(solution)/shard_map/ppermute | solution.py:18
  97.0 1.3 %collective-permute-start.1 = (bf16[1,2,32,64]{3,2,1,0:T(8,128)(2,1)S(1)}, bf16[1,2,32,64]{3,2,1,0:T(8,128)(2,1)S(1)}, u32[]{:S(2)}, u32[]{:S(2)}) collective-permute-start(bf16[1,2,32,64]{3,2,1,0:T(8,128)(2,1)S(1)} %bitcast.132), channel_id=1, source_target_pairs={{4,0},{8,4},{12,8},{5,1},{9,5},{13,9},{6,2},{10,6},{14,10},{7,3},{... | collective-permute-start | bytes 24584 | tf_op jit(solution)/shard_map/ppermute | solution.py:20
  98.3 0.1 collective-permute-done
  98.5 4.2 %collective-permute-done.1 = bf16[1,2,32,64]{3,2,1,0:T(8,128)(2,1)S(1)} collective-permute-done((bf16[1,2,32,64]{3,2,1,0:T(8,128)(2,1)S(1)}, bf16[1,2,32,64]{3,2,1,0:T(8,128)(2,1)S(1)}, u32[]{:S(2)}, u32[]{:S(2)}) %collective-permute-start.1) | collective-permute-done | bytes 8224 | tf_op jit(solution)/shard_map/ppermute | solution.py:20
  102.7 0.1 pad_maximum_fusion.1
  102.8 0.2 fusion.25
  103.0 0.2 convolution_add_fusion.1
  103.2 0.0 copy-done.6
  103.2 0.0 copy-done.3
  103.2 0.0 copy-start.5
  103.2 0.2 fusion.18
  103.5 0.1 pad_slice_fusion.1
  103.6 0.3 fusion.20
  103.8 0.3 convolution_add_fusion.3
  104.1 0.0 copy-done.5
  104.1 0.9 fusion.8
  (11 shorter events, 0.3 us)
Async XLA Ops:
  6.5 85.0 %copy-start = (bf16[4096,64]{0,1:T(8,128)(2,1)S(1)}, bf16[4096,64]{0,1:T(8,128)(2,1)}, u32[]{:S(2)}) copy-start(bf16[4096,64]{0,1:T(8,128)(2,1)} %param.14) | copy-start | bytes 1572868
  6.5 63.5 %all-gather.4.cloned.1.call-start = ((), (), s32[]{:S(2)}) async-start(), calls=%async_computation.4 | async-start | bytes 1310720 | tf_op jit(solution)/shard_map/all_gather | solution.py:118
  29.8 2.1 %copy-start.1 = (bf16[1,2,16,4096]{3,2,1,0:T(8,128)(2,1)S(1)}, bf16[1,2,16,4096]{3,2,1,0:T(8,128)(2,1)}, u32[]{:S(2)}) copy-start(bf16[1,2,16,4096]{3,2,1,0:T(8,128)(2,1)} %param.12) | copy-start | bytes 786436
  31.8 40.6 %all-gather.6.cloned.1.call-start = ((), (), s32[]{:S(2)}) async-start(), calls=%async_computation.5 | async-start | bytes 1310720 | tf_op jit(solution)/shard_map/all_gather | solution.py:119
  49.3 2.1 %copy-start.2 = (bf16[1,2,16,4096]{3,2,1,0:T(8,128)(2,1)S(1)}, bf16[1,2,16,4096]{3,2,1,0:T(8,128)(2,1)}, u32[]{:S(2)}) copy-start(bf16[1,2,16,4096]{3,2,1,0:T(8,128)(2,1)} %param.10) | copy-start | bytes 786436
  75.4 11.4 %all-to-all-start.3 = ((bf16[1,8,16,1024]{3,2,0,1:T(8,128)(2,1)}), bf16[1,8,16,1024]{3,2,0,1:T(8,128)(2,1)S(1)}, u32[]{:S(2)}, u32[]{:S(2)}) async-start(bf16[1,8,16,1024]{3,2,0,1:T(8,128)(2,1)} %bitcast.12), calls=%async_computation.3 | async-start | bytes 524288 | tf_op jit(solution)/shard_map/all_to_all | solution.py:124
  82.4 9.2 %copy-start.4 = (f32[4096]{0:T(1024)S(1)}, f32[4096]{0:T(1024)}, u32[]{:S(2)}) copy-start(f32[4096]{0:T(1024)} %param.13) | copy-start | bytes 49156
  90.8 12.4 %copy-start.6 = (f32[512]{0:T(512)S(1)}, f32[512]{0:T(512)}, u32[]{:S(2)}) copy-start(f32[512]{0:T(512)} %param.17) | copy-start | bytes 6148
  91.6 11.7 %copy-start.3 = (bf16[1,3,64,512]{3,2,1,0:T(8,128)(2,1)S(1)}, bf16[1,3,64,512]{3,2,1,0:T(8,128)(2,1)}, u32[]{:S(2)}) copy-start(bf16[1,3,64,512]{3,2,1,0:T(8,128)(2,1)} %get-tuple-element.8) | copy-start | bytes 589828
  94.8 3.7 %collective-permute-start = (bf16[1,2,32,64]{3,2,1,0:T(8,128)(2,1)S(1)}, bf16[1,2,32,64]{3,2,1,0:T(8,128)(2,1)S(1)}, u32[]{:S(2)}, u32[]{:S(2)}) collective-permute-start(bf16[1,2,32,64]{3,2,1,0:T(8,128)(2,1)S(1)} %bitcast.131), channel_id=1, source_target_pairs={{0,4},{4,8},{8,12},{1,5},{5,9},{9,13},{2,6},{6,10},{10,14},{3,7},{... | collective-permute-start | bytes 24584 | tf_op jit(solution)/shard_map/ppermute | solution.py:18
  97.0 5.6 %collective-permute-start.1 = (bf16[1,2,32,64]{3,2,1,0:T(8,128)(2,1)S(1)}, bf16[1,2,32,64]{3,2,1,0:T(8,128)(2,1)S(1)}, u32[]{:S(2)}, u32[]{:S(2)}) collective-permute-start(bf16[1,2,32,64]{3,2,1,0:T(8,128)(2,1)S(1)} %bitcast.132), channel_id=1, source_target_pairs={{4,0},{8,4},{12,8},{5,1},{9,5},{13,9},{6,2},{10,6},{14,10},{7,3},{... | collective-permute-start | bytes 24584 | tf_op jit(solution)/shard_map/ppermute | solution.py:20
  103.2 0.9 copy-start.5
Sparse Core Ops, SparseCore 0:
  32.0 15.7 all-gather.3
  51.5 15.7 all-gather.5
where the time goes:
time: 113 us; the launch traced here: 112 us
  blocking collectives  38.8 us (34%)
  local copies, waits for them, and re-layouts  34.3 us (30%)
  between operations  13.8 us (12%)
  waiting for transfers between devices  8.74 us (8%)
  matrix products  7.01 us (6%)
  starting transfers between devices  6.99 us (6%)
  other arithmetic  2.25 us (2%)
    unnamed x26, local copies, waits for them, and re-layouts  21.1 us
    all_to_all x1, blocking collectives, per_device(): lax.all_to_all(keys, 'seq', split_axis=3, concat_axis=1, tiled=True)  15 us
    all_to_all x1, blocking collectives, per_device(): lax.all_to_all(values, 'seq', split_axis=3, concat_axis=1, tiled=True)  11 us
    all_to_all x1, blocking collectives, per_device(): lax.all_to_all(queries, 'seq', split_axis=3, concat_axis=1, tiled=True)  11 us
    all_to_all x1, waiting for transfers between devices, per_device(): lax.all_to_all(attended, 'seq', split_axis=1, concat_axis=3, tiled=True)  4.35 us
    ppermute x1, waiting for transfers between devices, with_halo(): lax.ppermute(head, axis, [((i + 1) % count, i) for i in range(ends)])  4.21 us
    slice x2, local copies, waits for them, and re-layouts, conv_valid(): flat_kernel = kernel[row_tap].reshape(3 * kernel.shape[2], kernel.shape[3])  3.6 us
    all_to_all x1, starting transfers between devices, per_device(): lax.all_to_all(attended, 'seq', split_axis=1, concat_axis=3, tiled=True)  3.4 us
  transfers between devices with their start and end apart: 5, of which 3 were waited for; matrix products, arithmetic and copies ran while one was open for 20% of the time, Pallas kernels for 0%

commit v1 on v0

--- a/solution.py
+++ b/solution.py
@@ -5,6 +5,12 @@
 
 HD = 128
 epsilon = 1e-06
+
+
+def stacked_exchange(x, mesh_axis, split, join):
+    cells = jnp.split(x, lax.axis_size(mesh_axis), axis=split)
+    received = lax.all_to_all(jnp.stack(cells), mesh_axis, 0, 0)
+    return jnp.concatenate(received, axis=join)
 
 
 def with_halo(cells, sides, width):
@@ -80,7 +86,7 @@
     query_all, key_all, value_all = (
         lax.all_to_all(queries, "seq", split_axis=3, concat_axis=1, tiled=True),
         lax.all_to_all(keys, "seq", split_axis=3, concat_axis=1, tiled=True),
-        lax.all_to_all(values, "seq", split_axis=3, concat_axis=1, tiled=True),
+        stacked_exchange(values, "seq", 3, 1),
     )
     all_rows = query_all.shape[1]
 

time: 113 us -> 109 us (0.965)
  local copies, waits for them, and re-layouts: 34.3 us -> 26.7 us
  waiting for transfers between devices: 8.74 us -> 11.3 us
    unnamed x26 -> x23, local copies, waits for them, and re-layouts: 21.1 us -> 14.7 us
    all_to_all x1, waiting for transfers between devices: 4.35 us -> 5.68 us  [per_device(): lax.all_to_all(attended, 'seq', split_axis=1, concat_axis=3, tiled=True)]
    all_to_all x1 -> x0, local copies, waits for them, and re-layouts: 1.26 us -> none  [per_device(): lax.all_to_all(values, 'seq', split_axis=3, concat_axis=1, tiled=True)]
    all_gather x1, waiting for transfers between devices: 0.02 us -> 1.25 us  [per_device(): lax.all_gather(value_heads, ('blk', 'chan'), axis=1, tiled=True)]
    all_to_all x1, starting transfers between devices: 3.4 us -> 4.6 us  [per_device(): lax.all_to_all(attended, 'seq', split_axis=1, concat_axis=3, tiled=True)]
  transfers between devices with their start and end apart: 5 -> 5, of which waited for: 3 -> 4; matrix products, arithmetic and copies ran while one was open for 20% -> 13% of each run, Pallas kernels for 0% -> 0%
where the time goes in v1:
time: 109 us; the launch traced here: 108 us
  blocking collectives  38.8 us (36%)
  local copies, waits for them, and re-layouts  26.7 us (24%)
  between operations  13.7 us (13%)
  waiting for transfers between devices  11.3 us (10%)
  starting transfers between devices  7.85 us (7%)
  matrix products  7.01 us (6%)
  other arithmetic  2.29 us (2%)
    all_to_all x1, blocking collectives, per_device(): lax.all_to_all(keys, 'seq', split_axis=3, concat_axis=1, tiled=True)  15 us
    unnamed x23, local copies, waits for them, and re-layouts  14.7 us
    all_to_all x1, blocking collectives, per_device(): lax.all_to_all(queries, 'seq', split_axis=3, concat_axis=1, tiled=True)  11 us
    all_to_all x1, blocking collectives, stacked_exchange(): received = lax.all_to_all(jnp.stack(cells), mesh_axis, 0, 0)  11 us
    all_to_all x1, waiting for transfers between devices, per_device(): lax.all_to_all(attended, 'seq', split_axis=1, concat_axis=3, tiled=True)  5.68 us
    all_to_all x1, starting transfers between devices, per_device(): lax.all_to_all(attended, 'seq', split_axis=1, concat_axis=3, tiled=True)  4.6 us
    ppermute x1, waiting for transfers between devices, with_halo(): lax.ppermute(head, axis, [((i + 1) % count, i) for i in range(ends)])  4.21 us
    slice x2, local copies, waits for them, and re-layouts, conv_valid(): flat_kernel = kernel[row_tap].reshape(3 * kernel.shape[2], kernel.shape[3])  3.61 us
  transfers between devices with their start and end apart: 5, of which 4 were waited for; matrix products, arithmetic and copies ran while one was open for 13% of the time, Pallas kernels for 0%

profile of v1, /device:TPU:0, one launch (start us, length us, event | category | flops | bytes accessed | tf_op | source)
XLA Modules:
  0.0 107.7 jit_solution(1480210506293598384)
XLA Ops:
  6.5 0.0 copy-start
  6.5 0.0 all-gather.4.cloned.1.call-start
  6.5 4.5 %copy.27 = bf16[1,2,16,4096]{2,1,0,3:T(2,128)(2,1)S(1)} copy(bf16[1,2,16,4096]{3,2,1,0:T(8,128)(2,1)} %param.11) | data formatting | bytes 524288 | tf_op args[1]
  11.1 2.2 %reshape.136 = bf16[4,2,16384]{2,1,0:T(2,128)(2,1)S(1)} reshape(bf16[4096,1,2,16]{3,2,1,0:T(2,128)(2,1)S(1)} %bitcast.116) | data formatting | bytes 524288
  13.3 15.0 %all_to_all.44 = bf16[4,2,16384]{2,1,0:T(2,128)(2,1)S(1)} all-to-all(bf16[4,2,16384]{2,1,0:T(2,128)(2,1)S(1)} %reshape.136), channel_id=1, replica_groups=mesh['groups'=2,'seq'=4,'blk'=2,'chan'=2] {'seq'}, dimensions={0} | all-to-all | bytes 524288 | tf_op jit(solution)/shard_map/all_to_all | solution.py:88
  28.3 1.4 %reshape.137 = bf16[4096,1,2,16]{3,2,1,0:T(2,128)(2,1)S(1)} reshape(bf16[4,2,16384]{2,1,0:T(2,128)(2,1)S(1)} %all_to_all.44) | data formatting | bytes 524288
  29.8 0.0 copy-start.2
  29.8 1.3 %copy.28 = bf16[1,2,16,4,1024]{4,2,1,3,0:T(8,128)(2,1)S(1)} copy(bf16[1,2,16,4,1024]{2,1,4,3,0:T(2,128)(2,1)S(1)} %bitcast.114) | data formatting | bytes 524288 | tf_op jit(solution)/shard_map/all_to_all | solution.py:88
  31.0 0.0 copy-start.1
  31.1 0.7 copy.47
  31.8 0.0 all-gather.4.cloned.1.call-update
  31.9 0.0 all-gather.6.cloned.1.call-start
  31.9 0.0 copy-done.2
  32.0 11.0 %all_to_all.45 = bf16[4,1,2,16,1024]{4,3,2,1,0:T(8,128)(2,1)S(1)} all-to-all(bf16[4,1,2,16,1024]{4,3,2,1,0:T(8,128)(2,1)S(1)} %pad_maximum_fusion.1), channel_id=1, replica_groups=mesh['groups'=2,'seq'=4,'blk'=2,'chan'=2] {'seq'}, dimensions={0} | all-to-all | bytes 524288 | tf_op jit(solution)/shard_map/all_to_all | solution.py:12
  43.0 0.7 copy.46
  43.8 0.0 all-gather.6.cloned.1.call-update
  43.8 0.0 copy-done.1
  43.8 2.7 %copy.24 = bf16[1,2,16,4096]{2,1,0,3:T(2,128)(2,1)S(1)} copy(bf16[1,2,16,4096]{3,2,1,0:T(8,128)(2,1)S(1)} %copy-done.1) | data formatting | bytes 524288 | tf_op args[0]
  46.5 2.2 %reshape.138 = bf16[4,2,16384]{2,1,0:T(2,128)(2,1)S(1)} reshape(bf16[4096,1,2,16]{3,2,1,0:T(2,128)(2,1)S(1)} %bitcast.117) | data formatting | bytes 524288
  48.7 11.0 %all_to_all.46 = bf16[4,2,16384]{2,1,0:T(2,128)(2,1)S(1)} all-to-all(bf16[4,2,16384]{2,1,0:T(2,128)(2,1)S(1)} %reshape.138), channel_id=1, replica_groups=mesh['groups'=2,'seq'=4,'blk'=2,'chan'=2] {'seq'}, dimensions={0} | all-to-all | bytes 524288 | tf_op jit(solution)/shard_map/all_to_all | solution.py:87
  59.7 1.4 %reshape.139 = bf16[4096,1,2,16]{3,2,1,0:T(2,128)(2,1)S(1)} reshape(bf16[4,2,16384]{2,1,0:T(2,128)(2,1)S(1)} %all_to_all.46) | data formatting | bytes 524288
  61.2 1.3 %copy.25 = bf16[1,2,16,4,1024]{4,2,1,3,0:T(8,128)(2,1)S(1)} copy(bf16[1,2,16,4,1024]{2,1,4,3,0:T(2,128)(2,1)S(1)} %bitcast.115) | data formatting | bytes 524288 | tf_op jit(solution)/shard_map/all_to_all | solution.py:87
  62.5 0.0 all-gather.4.cloned.1.call-done
  62.5 1.8 %multiply_reduce_fusion = (f32[8,128]{1,0:T(8,128)S(1)}, f32[8,128,512]{2,1,0:T(8,128)S(1)}) fusion(bf16[8,512,128]{2,1,0:T(8,128)(2,1)} %all-gather.4.cloned.1.call-done, bf16[128,8,128]{2,1,0:T(8,128)(2,1)S(1)} %bitcast.129), kind=kOutput, calls=%fused_computation.1 | convolution fusion | flops 135265280 | bytes 3411968 | tf_op jit(solution)/shard_map/hqd,hkd->hqk/dot_general | solution.py:56
  64.3 0.6 fusion
  64.9 1.3 %all-gather.6.cloned.1.call-done = bf16[8,512,128]{2,1,0:T(8,128)(2,1)} async-done(((bf16[8,128,128]{2,1,0:T(8,128)(2,1)}), bf16[8,512,128]{2,1,0:T(8,128)(2,1)}) %all-gather.6.cloned.1.call-update) | async-done | bytes 1048592 | tf_op jit(solution)/shard_map/all_gather | solution.py:125
  66.1 1.9 %fusion.4 = bf16[128,8,128]{2,0,1:T(8,128)(2,1)S(1)} fusion(bf16[8,512,128]{2,1,0:T(8,128)(2,1)} %all-gather.6.cloned.1.call-done, f32[8,128,512]{2,1,0:T(8,128)S(1)} %get-tuple-element.22, f32[8,128]{1,0:T(8,128)S(1)} %get-tuple-element.20, f32[128,8]{0,1:T(8,128)S(1)} %bitcast_add_fusion, f32[128,8]{0,1:T(8,128)S(1)} %get-tuple-element.19), kind=kOutput, calls=%fused_computation.7 | convolution fusion | flops 136183808 | bytes 3420160 | tf_op jit(solution)/shard_map/hqk,hkd->hqd/dot_general | solution.py:63
  68.0 0.2 copy.31
  68.2 0.8 reshape.119
  69.0 4.6 %all-to-all-start.3 = ((bf16[1,8,16,1024]{3,2,0,1:T(8,128)(2,1)}), bf16[1,8,16,1024]{3,2,0,1:T(8,128)(2,1)S(1)}, u32[]{:S(2)}, u32[]{:S(2)}) async-start(bf16[1,8,16,1024]{3,2,0,1:T(8,128)(2,1)} %bitcast.14), calls=%async_computation.3 | async-start | bytes 524288 | tf_op jit(solution)/shard_map/all_to_all | solution.py:130
  73.6 1.8 %fusion.30 = (bf16[1,3,64,512]{3,2,1,0:T(8,128)(2,1)}, bf16[1,3,64,512]{3,2,1,0:T(8,128)(2,1)S(1)}, bf16[1,3,64,512]{3,2,1,0:T(8,128)(2,1)S(1)}) fusion(bf16[3,3,64,512]{3,2,1,0:T(8,128)(2,1)} %param.16), kind=kLoop, calls=%fused_computation.65 | loop fusion | bytes 1179648 | tf_op jit(solution)/shard_map/slice | solution.py:42
  75.5 1.8 %fusion.29 = (bf16[1,3,512,256]{3,2,1,0:T(8,128)(2,1)S(1)}, bf16[1,3,512,256]{3,2,1,0:T(8,128)(2,1)S(1)}, bf16[1,3,512,256]{3,2,1,0:T(8,128)(2,1)S(1)}) fusion(bf16[3,3,512,256]{3,2,1,0:T(8,128)(2,1)} %param.18), kind=kLoop, calls=%fused_computation.64 | loop fusion | bytes 4718592 | tf_op jit(solution)/shard_map/slice | solution.py:42
  77.2 0.0 copy-start.4
  77.2 5.7 %all-to-all-done.3 = bf16[1,8,16,1024]{3,2,0,1:T(8,128)(2,1)S(1)} async-done(((bf16[1,8,16,1024]{3,2,0,1:T(8,128)(2,1)}), bf16[1,8,16,1024]{3,2,0,1:T(8,128)(2,1)S(1)}, u32[]{:S(2)}, u32[]{:S(2)}) %all-to-all-start.3) | async-done | bytes 262176 | tf_op jit(solution)/shard_map/all_to_all | solution.py:130
  83.0 1.1 %copy.34 = f32[1,2,16,4,1024]{4,3,2,1,0:T(4,128)} copy(f32[1,2,16,4,1024]{4,2,1,3,0:T(8,128)S(1)} %bitcast.121) | data formatting | bytes 1048576 | tf_op jit(solution)/shard_map/convert_element_type | solution.py:131
  84.1 2.2 %reshape.126 = f32[2,16,4096]{2,1,0:T(8,128)} reshape(f32[1,2,16,4,1024]{4,3,2,1,0:T(4,128)} %copy.34) | data formatting | bytes 1048576 | tf_op jit(solution)/shard_map/convert_element_type | solution.py:131
  86.3 0.7 multiply_reduce_fusion.1
  87.0 0.0 copy-start.6
  87.0 0.7 reduce_sum.31
  87.8 0.0 copy-start.3
  87.8 0.0 copy-done
  87.8 0.0 copy-done.4
  87.8 1.4 %fusion.10 = bf16[2,16,64]{2,1,0:T(8,128)(2,1)S(1)} fusion(bf16[4096,64]{0,1:T(8,128)(2,1)S(1)} %copy-done, f32[2,16,4096]{2,1,0:T(8,128)} %reshape.126, f32[4096]{0:T(1024)S(1)} %copy-done.4, f32[64]{0:T(128)} %param.15, f32[2,16]{1,0:T(2,128)S(1)} %add_sqrt_fusion), kind=kOutput, calls=%fused_computation.18 | convolution fusion | flops 17045504 | bytes 1069440 | tf_op jit(solution)/shard_map/frcd,dl->frcl/dot_general | solution.py:134
  89.2 1.8 %all-gather = bf16[2,32,64]{2,1,0:T(8,128)(2,1)S(1)} all-gather(bf16[2,16,64]{2,1,0:T(8,128)(2,1)S(1)} %fusion.10), channel_id=2, replica_groups=mesh['groups'=2,'seq'=4,'blk'=2,'chan'=2] {'chan'}, dimensions={1}, use_global_device_ids=true | all-gather | bytes 12288 | tf_op jit(solution)/shard_map/all_gather | solution.py:137
  91.0 1.9 %collective-permute-start = (bf16[1,2,32,64]{3,2,1,0:T(8,128)(2,1)S(1)}, bf16[1,2,32,64]{3,2,1,0:T(8,128)(2,1)S(1)}, u32[]{:S(2)}, u32[]{:S(2)}) collective-permute-start(bf16[1,2,32,64]{3,2,1,0:T(8,128)(2,1)S(1)} %bitcast.133), channel_id=1, source_target_pairs={{0,4},{4,8},{8,12},{1,5},{5,9},{9,13},{2,6},{6,10},{10,14},{3,7},{... | collective-permute-start | bytes 24584 | tf_op jit(solution)/shard_map/ppermute | solution.py:24
  92.9 1.3 %collective-permute-start.1 = (bf16[1,2,32,64]{3,2,1,0:T(8,128)(2,1)S(1)}, bf16[1,2,32,64]{3,2,1,0:T(8,128)(2,1)S(1)}, u32[]{:S(2)}, u32[]{:S(2)}) collective-permute-start(bf16[1,2,32,64]{3,2,1,0:T(8,128)(2,1)S(1)} %bitcast.134), channel_id=1, source_target_pairs={{4,0},{8,4},{12,8},{5,1},{9,5},{13,9},{6,2},{10,6},{14,10},{7,3},{... | collective-permute-start | bytes 24584 | tf_op jit(solution)/shard_map/ppermute | solution.py:26
  94.2 0.1 collective-permute-done
  94.3 4.2 %collective-permute-done.1 = bf16[1,2,32,64]{3,2,1,0:T(8,128)(2,1)S(1)} collective-permute-done((bf16[1,2,32,64]{3,2,1,0:T(8,128)(2,1)S(1)}, bf16[1,2,32,64]{3,2,1,0:T(8,128)(2,1)S(1)}, u32[]{:S(2)}, u32[]{:S(2)}) %collective-permute-start.1) | collective-permute-done | bytes 8224 | tf_op jit(solution)/shard_map/ppermute | solution.py:26
  98.6 0.1 pad_maximum_fusion.2
  98.7 0.2 fusion.25
  98.9 0.2 convolution_add_fusion.1
  99.1 0.0 copy-done.6
  99.1 0.0 copy-done.3
  99.1 0.0 copy-start.5
  99.1 0.2 fusion.18
  99.4 0.1 pad_slice_fusion.1
  99.5 0.3 fusion.20
  99.7 0.3 convolution_add_fusion.3
  100.0 0.0 copy-done.5
  100.0 0.9 fusion.8
  (13 shorter events, 0.3 us)
Async XLA Ops:
  6.5 81.2 %copy-start = (bf16[4096,64]{0,1:T(8,128)(2,1)S(1)}, bf16[4096,64]{0,1:T(8,128)(2,1)}, u32[]{:S(2)}) copy-start(bf16[4096,64]{0,1:T(8,128)(2,1)} %param.14) | copy-start | bytes 1572868
  6.5 56.0 %all-gather.4.cloned.1.call-start = ((), (), s32[]{:S(2)}) async-start(), calls=%async_computation.4 | async-start | bytes 1310720 | tf_op jit(solution)/shard_map/all_gather | solution.py:124
  29.8 2.2 %copy-start.2 = (bf16[1,2,16,4096]{3,2,1,0:T(8,128)(2,1)S(1)}, bf16[1,2,16,4096]{3,2,1,0:T(8,128)(2,1)}, u32[]{:S(2)}) copy-start(bf16[1,2,16,4096]{3,2,1,0:T(8,128)(2,1)} %param.12) | copy-start | bytes 786436
  31.0 12.8 %copy-start.1 = (bf16[1,2,16,4096]{3,2,1,0:T(8,128)(2,1)S(1)}, bf16[1,2,16,4096]{3,2,1,0:T(8,128)(2,1)}, u32[]{:S(2)}) copy-start(bf16[1,2,16,4096]{3,2,1,0:T(8,128)(2,1)} %param.10) | copy-start | bytes 786436
  31.9 34.3 %all-gather.6.cloned.1.call-start = ((), (), s32[]{:S(2)}) async-start(), calls=%async_computation.5 | async-start | bytes 1310720 | tf_op jit(solution)/shard_map/all_gather | solution.py:125
  69.0 13.9 %all-to-all-start.3 = ((bf16[1,8,16,1024]{3,2,0,1:T(8,128)(2,1)}), bf16[1,8,16,1024]{3,2,0,1:T(8,128)(2,1)S(1)}, u32[]{:S(2)}, u32[]{:S(2)}) async-start(bf16[1,8,16,1024]{3,2,0,1:T(8,128)(2,1)} %bitcast.14), calls=%async_computation.3 | async-start | bytes 524288 | tf_op jit(solution)/shard_map/all_to_all | solution.py:130
  77.2 10.6 %copy-start.4 = (f32[4096]{0:T(1024)S(1)}, f32[4096]{0:T(1024)}, u32[]{:S(2)}) copy-start(f32[4096]{0:T(1024)} %param.13) | copy-start | bytes 49156
  87.0 12.0 %copy-start.6 = (f32[512]{0:T(512)S(1)}, f32[512]{0:T(512)}, u32[]{:S(2)}) copy-start(f32[512]{0:T(512)} %param.17) | copy-start | bytes 6148
  87.8 11.3 %copy-start.3 = (bf16[1,3,64,512]{3,2,1,0:T(8,128)(2,1)S(1)}, bf16[1,3,64,512]{3,2,1,0:T(8,128)(2,1)}, u32[]{:S(2)}) copy-start(bf16[1,3,64,512]{3,2,1,0:T(8,128)(2,1)} %get-tuple-element.8) | copy-start | bytes 589828
  91.0 3.4 %collective-permute-start = (bf16[1,2,32,64]{3,2,1,0:T(8,128)(2,1)S(1)}, bf16[1,2,32,64]{3,2,1,0:T(8,128)(2,1)S(1)}, u32[]{:S(2)}, u32[]{:S(2)}) collective-permute-start(bf16[1,2,32,64]{3,2,1,0:T(8,128)(2,1)S(1)} %bitcast.133), channel_id=1, source_target_pairs={{0,4},{4,8},{8,12},{1,5},{5,9},{9,13},{2,6},{6,10},{10,14},{3,7},{... | collective-permute-start | bytes 24584 | tf_op jit(solution)/shard_map/ppermute | solution.py:24
  92.9 5.6 %collective-permute-start.1 = (bf16[1,2,32,64]{3,2,1,0:T(8,128)(2,1)S(1)}, bf16[1,2,32,64]{3,2,1,0:T(8,128)(2,1)S(1)}, u32[]{:S(2)}, u32[]{:S(2)}) collective-permute-start(bf16[1,2,32,64]{3,2,1,0:T(8,128)(2,1)S(1)} %bitcast.134), channel_id=1, source_target_pairs={{4,0},{8,4},{12,8},{5,1},{9,5},{13,9},{6,2},{10,6},{14,10},{7,3},{... | collective-permute-start | bytes 24584 | tf_op jit(solution)/shard_map/ppermute | solution.py:26
  99.1 0.9 copy-start.5
Sparse Core Ops, SparseCore 0:
  32.0 15.7 all-gather.3
  49.4 16.6 all-gather.5
